TPU v7x, 32 devices: a whole 2x2x4 slice. The times are simulated.
32 devices in a mesh: dp: 4 (over z), blk: 8 (over y, x, core).
Axes of the slice: x: 2, y: 2, z: 4, core: 2. Of those that a mesh axis runs over, the one named last changes fastest.
Arguments:
- tokens: bfloat16 [4096, 768], P(('dp', 'blk')), may hold values from -6 to 6
- attn_gain: float32 [768], P(('dp', 'blk')), may hold values from 0.5 to 1.5
- q_weight: float32 [768, 768], P(('dp', 'blk')), may hold values from -0.21875 to 0.21875
- k_weight: float32 [768, 768], P(('dp', 'blk')), may hold values from -0.21875 to 0.21875
- v_weight: float32 [768, 768], P(('dp', 'blk')), may hold values from -0.21875 to 0.21875
- o_weight: float32 [768, 768], P(('dp', 'blk')), may hold values from -1.75 to 1.75
- mlp_gain: float32 [768], P(('dp', 'blk')), may hold values from 0.5 to 1.5
- gate_weight: float32 [768, 3072], P(('dp', 'blk')), may hold values from -0.21875 to 0.21875
- up_weight: float32 [768, 3072], P(('dp', 'blk')), may hold values from -0.21875 to 0.21875
- down_weight: float32 [3072, 768], P(('dp', 'blk')), may hold values from -0.109375 to 0.109375
- doc_lengths: int32 [4, 8], P('dp'), may hold values from 0 to 1024, as said below
- keep: int32 [4096], P(('dp', 'blk')), may hold values 0 or 1
- cotangent: bfloat16 [4096, 768], P(('dp', 'blk')), may hold values from -6 to 6
Outputs:
- layer_out: bfloat16 [4096, 768], P(('dp', 'blk'))
- tokens_grad: bfloat16 [4096, 768], P(('dp', 'blk'))
- attn_gain_grad: float32 [768], P(('dp', 'blk'))
- q_grad: float32 [768, 768], P(('dp', 'blk'))
- k_grad: float32 [768, 768], P(('dp', 'blk'))
- v_grad: float32 [768, 768], P(('dp', 'blk'))
- o_grad: float32 [768, 768], P(('dp', 'blk'))
- mlp_gain_grad: float32 [768], P(('dp', 'blk'))
- gate_grad: float32 [768, 3072], P(('dp', 'blk'))
- up_grad: float32 [768, 3072], P(('dp', 'blk'))
- down_grad: float32 [3072, 768], P(('dp', 'blk'))
Inputs may be any that keep to these rules, and one draw needn't show every extreme that they name: `doc_lengths`: each row lists its documents' lengths in order, then zeros; every length is 128, 512 or 1024, and a row's lengths sum to 1024. In every draw some row is a single document of 1024 tokens.
All inputs are finite; a program needn't handle non-finite values. No bound on the sum of `keep` on one device may be relied on, other than what follows from the above.
Results may differ from a plain program's by a relative error of at most 0.014.
The roundings to bfloat16 on the way count: a program that leaves them out, or rounds other values in their place, can miss the bound.
Values may be sent and summed in bfloat16 or wider, within the bound.
A program may use at most 192 MiB of HBM per device.

v0:
```python
import math

import jax
import jax.numpy as jnp
from jax import lax
from jax.sharding import PartitionSpec as P

H = 12
KVH = 12
HD = 64


EPS = 1e-05
THETA = 10000.0
NEG = -1e30


def angles(in_doc):
    half = HD // 2
    freq = jnp.power(THETA, -jnp.arange(half, dtype=jnp.float32) * 2.0 / HD)
    phase = in_doc.astype(jnp.float32)[:, None] * freq[None, :]
    return (jnp.cos(phase)[:, None, :], jnp.sin(phase)[:, None, :])


def turn(values, cosine, sine):
    count = values.shape[0]
    shaped = values.reshape(count, -1, HD)
    half = HD // 2
    first = shaped[:, :, :half]
    second = shaped[:, :, half:]
    turned = jnp.concatenate(
        [first * cosine - second * sine, second * cosine + first * sine], axis=-1
    )
    return turned.reshape(count, -1)


def block_scores(queries, key_block, start_key, qpos, begin, scale):
    keys = key_block.reshape(-1, KVH, HD)
    raw = jnp.einsum("qkgd,skd->kgqs", queries, keys, preferred_element_type=jnp.float32) * scale
    kpos = start_key + jnp.arange(key_block.shape[0], dtype=jnp.int32)
    allow = (kpos[None, :] <= qpos[:, None]) & (kpos[None, :] >= begin[:, None])
    return (raw, allow)


def body(
    tokens,
    attn_gain,
    q_weight,
    k_weight,
    v_weight,
    o_weight,
    mlp_gain,
    gate_weight,
    up_weight,
    down_weight,
    doc_lengths,
    keep,
    cotangent,
):
    count = tokens.shape[0]
    group = H // KVH
    scale = 1.0 / math.sqrt(HD)
    cycle = lax.axis_size("blk")
    row_len = count * cycle
    kblock = min(512, row_len)
    nblocks = row_len // kblock
    qpos = lax.axis_index("blk") * count + jnp.arange(count, dtype=jnp.int32)
    lengths = doc_lengths[0]
    ends = jnp.cumsum(lengths)
    starts = ends - lengths
    inside = (qpos[:, None] >= starts[None, :]) & (qpos[:, None] < ends[None, :])
    begin = jnp.sum(jnp.where(inside, starts[None, :], 0), axis=-1)
    cosine, sine = angles(qpos - begin)
    keep_f = keep.astype(jnp.float32)[:, None]
    inputs = tokens.astype(jnp.float32)
    scale1 = lax.rsqrt(jnp.mean(inputs * inputs, axis=-1, keepdims=True) + EPS)
    unit1 = inputs * scale1
    gain_piece = lax.all_gather(attn_gain.astype(jnp.bfloat16), ("dp", "blk"), axis=0, tiled=True)
    q_piece = lax.all_gather(q_weight.astype(jnp.bfloat16), ("dp", "blk"), axis=0, tiled=True)
    k_piece = lax.all_gather(k_weight.astype(jnp.bfloat16), ("dp", "blk"), axis=0, tiled=True)
    v_piece = lax.all_gather(v_weight.astype(jnp.bfloat16), ("dp", "blk"), axis=0, tiled=True)
    cols = unit1
    gain_f = gain_piece.astype(jnp.float32)
    piece_norm = (cols * gain_f[None, :]).astype(jnp.bfloat16)
    q_acc = jnp.dot(piece_norm, q_piece, preferred_element_type=jnp.float32)
    k_acc = jnp.dot(piece_norm, k_piece, preferred_element_type=jnp.float32)
    v_acc = jnp.dot(piece_norm, v_piece, preferred_element_type=jnp.float32)
    normed = piece_norm
    gains = gain_f
    q_acc, k_acc, v_acc, normed1, gains1 = (q_acc, k_acc, v_acc, normed, gains)
    q_rot = turn(q_acc, cosine, sine).astype(jnp.bfloat16)
    k_rot = turn(k_acc, cosine, sine).astype(jnp.bfloat16)
    v_low = v_acc.astype(jnp.bfloat16)
    keys_all, values_all = (
        lax.all_gather(k_rot, "blk", axis=0, tiled=True),
        lax.all_gather(v_low, "blk", axis=0, tiled=True),
    )
    queries = q_rot.reshape(count, KVH, group, HD)
    block_starts = jnp.arange(nblocks, dtype=jnp.int32) * kblock
    key_blocks = keys_all.reshape(nblocks, kblock, KVH * HD)
    value_blocks = values_all.reshape(nblocks, kblock, KVH * HD)

    def stats_step(carry, item):
        top, total = carry
        key_block, start_key = item
        raw, allow = block_scores(queries, key_block, start_key, qpos, begin, scale)
        masked = jnp.where(allow, raw, NEG)
        new_top = jnp.maximum(top, jnp.max(masked, axis=-1))
        expo = jnp.where(allow, jnp.exp(masked - new_top[..., None]), 0.0)
        total = total * jnp.exp(top - new_top) + jnp.sum(expo, axis=-1)
        return ((new_top, total), None)

    start_stats = (
        jnp.full((KVH, group, count), NEG, jnp.float32),
        jnp.zeros((KVH, group, count), jnp.float32),
    )
    (top, total), unused = lax.scan(stats_step, start_stats, (key_blocks, block_starts))
    log_total = top + jnp.log(total)

    def value_step(acc, item):
        key_block, value_block, start_key = item
        raw, allow = block_scores(queries, key_block, start_key, qpos, begin, scale)
        probs = jnp.where(allow, jnp.exp(raw - log_total[..., None]), 0.0).astype(jnp.bfloat16)
        vals = value_block.reshape(-1, KVH, HD)
        acc = acc + jnp.einsum("kgqs,skd->qkgd", probs, vals, preferred_element_type=jnp.float32)
        return (acc, None)

    mixed_acc, unused = lax.scan(
        value_step,
        jnp.zeros((count, KVH, group, HD), jnp.float32),
        (key_blocks, value_blocks, block_starts),
    )
    mixed = mixed_acc.reshape(count, H * HD).astype(jnp.bfloat16)
    cols = mixed
    branch = jnp.dot(
        cols,
        lax.all_gather(o_weight.astype(jnp.bfloat16), ("dp", "blk"), axis=0, tiled=True),
        preferred_element_type=jnp.float32,
    )
    hidden_state = inputs + keep_f * branch
    scale2 = lax.rsqrt(jnp.mean(hidden_state * hidden_state, axis=-1, keepdims=True) + EPS)
    unit2 = hidden_state * scale2
    gain_piece = lax.all_gather(mlp_gain.astype(jnp.bfloat16), ("dp", "blk"), axis=0, tiled=True)
    gate_piece = lax.all_gather(gate_weight.astype(jnp.bfloat16), ("dp", "blk"), axis=0, tiled=True)
    up_piece = lax.all_gather(up_weight.astype(jnp.bfloat16), ("dp", "blk"), axis=0, tiled=True)
    cols = unit2
    gain_f = gain_piece.astype(jnp.float32)
    piece_norm = (cols * gain_f[None, :]).astype(jnp.bfloat16)
    gate_acc = jnp.dot(piece_norm, gate_piece, preferred_element_type=jnp.float32)
    up_acc = jnp.dot(piece_norm, up_piece, preferred_element_type=jnp.float32)
    normed = piece_norm
    gains = gain_f
    sig = jax.nn.sigmoid(gate_acc)
    hidden = (gate_acc * sig * up_acc).astype(jnp.bfloat16)
    down_whole = lax.all_gather(down_weight.astype(jnp.bfloat16), ("dp", "blk"), axis=0, tiled=True)
    result = jnp.dot(hidden, down_whole, preferred_element_type=jnp.float32)
    layer_out = (hidden_state + keep_f * result).astype(jnp.bfloat16)
    grad_out = cotangent.astype(jnp.float32)
    grad_y = (keep_f * grad_out).astype(jnp.bfloat16)
    grad_hidden = jnp.einsum("tc,nc->tn", grad_y, down_whole, preferred_element_type=jnp.float32)
    cols = hidden
    down_grad = lax.psum_scatter(
        jnp.einsum("tn,tc->nc", cols, grad_y, preferred_element_type=jnp.float32),
        ("dp", "blk"),
        scatter_dimension=0,
        tiled=True,
    )
    grad_gate = (grad_hidden * up_acc * sig * (1.0 + gate_acc * (1.0 - sig))).astype(jnp.bfloat16)
    grad_up = (grad_hidden * gate_acc * sig).astype(jnp.bfloat16)
    gate_piece, up_piece = lax.all_gather(
        (gate_weight.astype(jnp.bfloat16), up_weight.astype(jnp.bfloat16)),
        ("dp", "blk"),
        axis=0,
        tiled=True,
    )
    part_gate = jnp.einsum("tf,nf->tn", grad_gate, gate_piece, preferred_element_type=jnp.float32)
    part_up = jnp.einsum("tf,nf->tn", grad_up, up_piece, preferred_element_type=jnp.float32)
    grad_norm2 = part_gate + part_up
    mlp_gain_local = jnp.sum(grad_norm2 * unit2, axis=0)
    grad_unit2 = grad_norm2 * gains[None, :]
    grad_state = grad_out + scale2 * (
        grad_unit2 - unit2 * jnp.mean(grad_unit2 * unit2, axis=-1, keepdims=True)
    )
    grad_branch = (keep_f * grad_state).astype(jnp.bfloat16)
    grad_mixed = jnp.einsum(
        "tc,nc->tn",
        grad_branch,
        lax.all_gather(o_weight.astype(jnp.bfloat16), ("dp", "blk"), axis=0, tiled=True),
        preferred_element_type=jnp.float32,
    ).astype(jnp.bfloat16)
    grad_heads = grad_mixed.reshape(count, KVH, group, HD)

    def delta_step(acc, item):
        key_block, value_block, start_key = item
        raw, allow = block_scores(queries, key_block, start_key, qpos, begin, scale)
        probs = jnp.where(allow, jnp.exp(raw - log_total[..., None]), 0.0)
        vals = value_block.reshape(-1, KVH, HD)
        grad_probs = jnp.einsum(
            "qkgd,skd->kgqs", grad_heads, vals, preferred_element_type=jnp.float32
        )
        return (acc + jnp.sum(probs * grad_probs, axis=-1), None)

    delta, unused = lax.scan(
        delta_step,
        jnp.zeros((KVH, group, count), jnp.float32),
        (key_blocks, value_blocks, block_starts),
    )

    def grad_step(dq_acc, item):
        key_block, value_block, start_key = item
        raw, allow = block_scores(queries, key_block, start_key, qpos, begin, scale)
        probs = jnp.where(allow, jnp.exp(raw - log_total[..., None]), 0.0)
        keys = key_block.reshape(-1, KVH, HD)
        vals = value_block.reshape(-1, KVH, HD)
        grad_probs = jnp.einsum(
            "qkgd,skd->kgqs", grad_heads, vals, preferred_element_type=jnp.float32
        )
        grad_scores = (probs * (grad_probs - delta[..., None]) * scale).astype(jnp.bfloat16)
        dq_acc = dq_acc + jnp.einsum(
            "kgqs,skd->qkgd", grad_scores, keys, preferred_element_type=jnp.float32
        )
        dk_block = jnp.einsum(
            "kgqs,qkgd->skd", grad_scores, queries, preferred_element_type=jnp.float32
        )
        dv_block = jnp.einsum(
            "kgqs,qkgd->skd",
            probs.astype(jnp.bfloat16),
            grad_heads,
            preferred_element_type=jnp.float32,
        )
        return (dq_acc, (dk_block, dv_block))

    dq_acc, (dk_blocks, dv_blocks) = lax.scan(
        grad_step,
        jnp.zeros((count, KVH, group, HD), jnp.float32),
        (key_blocks, value_blocks, block_starts),
    )
    dk_term = dk_blocks.reshape(row_len, KVH * HD)
    dv_term = dv_blocks.reshape(row_len, KVH * HD)
    dk_sum, dv_sum = (
        lax.psum_scatter(
            dk_term.astype(jnp.bfloat16), "blk", scatter_dimension=0, tiled=True
        ).astype(jnp.float32),
        lax.psum_scatter(
            dv_term.astype(jnp.bfloat16), "blk", scatter_dimension=0, tiled=True
        ).astype(jnp.float32),
    )
    grad_q = turn(dq_acc.reshape(count, H * HD), cosine, -sine).astype(jnp.bfloat16)
    grad_k = turn(dk_sum, cosine, -sine).astype(jnp.bfloat16)
    grad_v = dv_sum.astype(jnp.bfloat16)
    q_piece, k_piece, v_piece = lax.all_gather(
        (
            q_weight.astype(jnp.bfloat16),
            k_weight.astype(jnp.bfloat16),
            v_weight.astype(jnp.bfloat16),
        ),
        ("dp", "blk"),
        axis=0,
        tiled=True,
    )
    part_q = jnp.einsum("tc,nc->tn", grad_q, q_piece, preferred_element_type=jnp.float32)
    part_k = jnp.einsum("tc,nc->tn", grad_k, k_piece, preferred_element_type=jnp.float32)
    part_v = jnp.einsum("tc,nc->tn", grad_v, v_piece, preferred_element_type=jnp.float32)
    grad_norm1 = part_q + part_k + part_v
    attn_gain_local = jnp.sum(grad_norm1 * unit1, axis=0)
    out_term = jnp.einsum("tn,tc->nc", mixed, grad_branch, preferred_element_type=jnp.float32)
    q_term = jnp.einsum("tn,tc->nc", normed1, grad_q, preferred_element_type=jnp.float32)
    k_term = jnp.einsum("tn,tc->nc", normed1, grad_k, preferred_element_type=jnp.float32)
    v_term = jnp.einsum("tn,tc->nc", normed1, grad_v, preferred_element_type=jnp.float32)
    gate_term = jnp.einsum("tn,tf->nf", normed, grad_gate, preferred_element_type=jnp.float32)
    up_term = jnp.einsum("tn,tf->nf", normed, grad_up, preferred_element_type=jnp.float32)
    attn_gain_grad, mlp_gain_grad, o_grad, q_grad, k_grad, v_grad, gate_grad, up_grad = (
        lax.psum_scatter(
            (attn_gain_local, mlp_gain_local, out_term, q_term, k_term, v_term, gate_term, up_term),
            ("dp", "blk"),
            scatter_dimension=0,
            tiled=True,
        )
    )
    grad_unit1 = grad_norm1 * gains1[None, :]
    tokens_grad = grad_state + scale1 * (
        grad_unit1 - unit1 * jnp.mean(grad_unit1 * unit1, axis=-1, keepdims=True)
    )
    return (
        layer_out,
        tokens_grad.astype(jnp.bfloat16),
        attn_gain_grad,
        q_grad,
        k_grad,
        v_grad,
        o_grad,
        mlp_gain_grad,
        gate_grad,
        up_grad,
        down_grad,
    )


def solution(mesh):
    in_specs = (
        P(("dp", "blk"), None),
        P(("dp", "blk")),
        P(("dp", "blk"), None),
        P(("dp", "blk"), None),
        P(("dp", "blk"), None),
        P(("dp", "blk"), None),
        P(("dp", "blk")),
        P(("dp", "blk"), None),
        P(("dp", "blk"), None),
        P(("dp", "blk"), None),
        P("dp", None),
        P(("dp", "blk")),
        P(("dp", "blk"), None),
    )
    out_specs = (
        P(("dp", "blk"), None),
        P(("dp", "blk"), None),
        P(("dp", "blk")),
        P(("dp", "blk"), None),
        P(("dp", "blk"), None),
        P(("dp", "blk"), None),
        P(("dp", "blk"), None),
        P(("dp", "blk")),
        P(("dp", "blk"), None),
        P(("dp", "blk"), None),
        P(("dp", "blk"), None),
    )
    return jax.shard_map(body, mesh=mesh, in_specs=in_specs, out_specs=out_specs, check_vma=False)
```

profile of v0, /device:TPU:0, one launch (start us, length us, event | category | flops | bytes accessed | tf_op | source)
XLA Modules:
  0.0 1479.1 jit_solution(6435042691247872890)
XLA Ops:
  13.7 42.1 %all-reduce.5 = (bf16[768]{0:T(1024)(128)(2,1)S(1)}, bf16[768]{0:T(1024)(128)(2,1)S(1)}) all-reduce(bf16[768]{0:T(1024)(128)(2,1)S(1)} %dynamic-update-slice, bf16[768]{0:T(1024)(128)(2,1)S(1)} %dynamic-update-slice.1), channel_id=1, replica_groups=mesh['dp'=4,'blk'=8] {'dp','blk'}, use_global_device_ids=true, to_apply=%add | all-reduce | flops 1536 | bytes 6144
  60.4 7.9 all-gather.14.cloned.1.call-done
  70.3 54.5 %all-gather.18.cloned.1.call-done = bf16[768,768]{1,0:T(8,128)(2,1)} async-done(((bf16[24,768]{1,0:T(8,128)(2,1)}), bf16[768,768]{1,0:T(8,128)(2,1)}) %all-gather.18.cloned.1.call-update) | async-done | bytes 1179664 | tf_op jit(solution)/shard_map/all_gather | solution.py:79
  127.8 53.5 %all-gather.10.cloned.1.call-done = bf16[768,768]{1,0:T(8,128)(2,1)} async-done(((bf16[24,768]{1,0:T(8,128)(2,1)}), bf16[768,768]{1,0:T(8,128)(2,1)}) %all-gather.10.cloned.1.call-update) | async-done | bytes 1179664 | tf_op jit(solution)/shard_map/all_gather | solution.py:81
  188.4 19.9 %all-gather.16.cloned.1.call-done = bf16[1024,768]{1,0:T(8,128)(2,1)} async-done(((bf16[128,768]{1,0:T(8,128)(2,1)}), bf16[1024,768]{1,0:T(8,128)(2,1)}) %all-gather.16.cloned.1.call-update) | async-done | bytes 1572880 | tf_op jit(solution)/shard_map/all_gather | solution.py:95
  210.8 25.4 %all-gather.12.cloned.1.call-done = bf16[1024,768]{1,0:T(8,128)(2,1)} async-done(((bf16[128,768]{1,0:T(8,128)(2,1)}), bf16[1024,768]{1,0:T(8,128)(2,1)}) %all-gather.12.cloned.1.call-update) | async-done | bytes 1572880 | tf_op jit(solution)/shard_map/all_gather | solution.py:96
  238.9 14.0 while.50
  253.6 12.4 while.51
  267.1 26.6 %all-gather.20.cloned.1.call-done = bf16[768,768]{1,0:T(8,128)(2,1)} async-done(((bf16[24,768]{1,0:T(8,128)(2,1)}), bf16[768,768]{1,0:T(8,128)(2,1)}) %all-gather.20.cloned.1.call-update) | async-done | bytes 1179664 | tf_op jit(solution)/shard_map/all_gather | solution.py:137
  295.6 64.2 %all-gather.24.cloned.1.call-done = bf16[768,3072]{1,0:T(8,128)(2,1)} async-done(((bf16[24,3072]{1,0:T(8,128)(2,1)}), bf16[768,3072]{1,0:T(8,128)(2,1)}) %all-gather.24.cloned.1.call-update) | async-done | bytes 4718608 | tf_op jit(solution)/shard_map/all_gather | solution.py:145
  364.0 61.7 %all-gather.22.cloned.1.call-done = bf16[768,3072]{1,0:T(8,128)(2,1)} async-done(((bf16[24,3072]{1,0:T(8,128)(2,1)}), bf16[768,3072]{1,0:T(8,128)(2,1)}) %all-gather.22.cloned.1.call-update) | async-done | bytes 4718608 | tf_op jit(solution)/shard_map/all_gather | solution.py:144
  430.0 61.7 %all-gather.26.cloned.1.call-done = bf16[3072,768]{1,0:T(8,128)(2,1)} async-done(((bf16[96,768]{1,0:T(8,128)(2,1)}), bf16[3072,768]{1,0:T(8,128)(2,1)}) %all-gather.26.cloned.1.call-update) | async-done | bytes 4718608 | tf_op jit(solution)/shard_map/all_gather | solution.py:155
  504.7 13.6 while.52
  518.4 27.9 %while.53 = (s32[]{:T(128)}, f32[128,12,1,64]{0,3,1,2:T(8,128)S(1)}, bf16[2,512,12,64]{1,3,2,0:T(8,128)(2,1)}, bf16[2,512,12,64]{1,3,2,0:T(8,128)(2,1)}, bf16[2,...) while((s32[]{:T(128)}, ...), condition=%wide.region_15.16_spmd.clone, body=%wide.region_14.15_spmd.clone.sunk | while | flops 512361088 | bytes 51678092 | solution.py:233
  558.4 30.3 %reduce-scatter.28.cloned.1.call-done = bf16[128,768]{1,0:T(8,128)(2,1)} async-done(((bf16[1024,768]{1,0:T(8,128)(2,1)}), bf16[128,768]{1,0:T(8,128)(2,1)}) %reduce-scatter.28.cloned.1.call-update) | async-done | bytes 196624
  594.2 36.3 %reduce-scatter.30.cloned.1.call-done = bf16[128,768]{1,0:T(8,128)(2,1)} async-done(((bf16[1024,768]{1,0:T(8,128)(2,1)}), bf16[128,768]{1,0:T(8,128)(2,1)}) %reduce-scatter.30.cloned.1.call-update) | async-done | bytes 196624
  657.8 39.8 %all-reduce.4 = (f32[768]{0:T(1024)S(1)}, f32[768]{0:T(1024)S(1)}) all-reduce(f32[768]{0:T(1024)S(1)} %get-tuple-element.527, f32[768]{0:T(1024)S(1)} %get-tuple-element.525), channel_id=4, replica_groups=mesh['dp'=4,'blk'=8] {'dp','blk'}, use_global_device_ids=true, to_apply=%region_20.21.clone | all-reduce | flops 1536 | bytes 12288
  699.6 35.6 %reduce-scatter.20.cloned.1.call-done = f32[24,768]{1,0:T(8,128)} async-done(((f32[768,768]{1,0:T(8,128)}), f32[24,768]{1,0:T(8,128)}) %reduce-scatter.20.cloned.1.call-update) | async-done | bytes 73744 | tf_op jit(solution)/shard_map/reduce_scatter | solution.py:273
  735.2 104.8 %reduce-scatter.14.cloned.1.call-done = f32[24,768]{1,0:T(8,128)} async-done(((f32[768,768]{1,0:T(8,128)}), f32[24,768]{1,0:T(8,128)}) %reduce-scatter.14.cloned.1.call-update) | async-done | bytes 73744 | tf_op jit(solution)/shard_map/reduce_scatter | solution.py:273
  840.0 103.8 %reduce-scatter.16.cloned.1.call-done = f32[24,768]{1,0:T(8,128)} async-done(((f32[768,768]{1,0:T(8,128)}), f32[24,768]{1,0:T(8,128)}) %reduce-scatter.16.cloned.1.call-update) | async-done | bytes 73744 | tf_op jit(solution)/shard_map/reduce_scatter | solution.py:273
  943.8 104.5 %reduce-scatter.18.cloned.1.call-done = f32[24,768]{1,0:T(8,128)} async-done(((f32[768,768]{1,0:T(8,128)}), f32[24,768]{1,0:T(8,128)}) %reduce-scatter.18.cloned.1.call-update) | async-done | bytes 73744 | tf_op jit(solution)/shard_map/reduce_scatter | solution.py:273
  1048.3 141.1 %reduce-scatter.22.cloned.1.call-done = f32[24,3072]{1,0:T(8,128)} async-done(((f32[768,3072]{1,0:T(8,128)}), f32[24,3072]{1,0:T(8,128)}) %reduce-scatter.22.cloned.1.call-update) | async-done | bytes 294928 | tf_op jit(solution)/shard_map/reduce_scatter | solution.py:273
  1189.4 141.8 %reduce-scatter.24.cloned.1.call-done = f32[24,3072]{1,0:T(8,128)} async-done(((f32[768,3072]{1,0:T(8,128)}), f32[24,3072]{1,0:T(8,128)}) %reduce-scatter.24.cloned.1.call-update) | async-done | bytes 294928 | tf_op jit(solution)/shard_map/reduce_scatter | solution.py:273
  1331.2 141.1 %reduce-scatter.26.cloned.1.call-done = f32[96,768]{1,0:T(8,128)} async-done(((f32[3072,768]{1,0:T(8,128)}), f32[96,768]{1,0:T(8,128)}) %reduce-scatter.26.cloned.1.call-update) | async-done | bytes 294928 | tf_op jit(solution)/shard_map/reduce_scatter | solution.py:162
  (316 shorter events, 166.9 us)
Async XLA Ops:
  7.2 117.6 %copy-start.2 = (bf16[128,768]{1,0:T(8,128)(2,1)S(1)}, bf16[128,768]{1,0:T(8,128)(2,1)}, u32[]{:S(2)}) copy-start(bf16[128,768]{1,0:T(8,128)(2,1)} %param.21) | copy-start | bytes 589828
  7.2 61.1 %all-gather.14.cloned.1.call-start = ((), (), s32[]{:S(2)}) async-start(), calls=%async_computation.11 | async-start | bytes 1216512 | tf_op jit(solution)/shard_map/all_gather | solution.py:80
  8.8 116.0 %all-gather.18.cloned.1.call-start = ((), (), s32[]{:S(2)}) async-start(), calls=%async_computation.13 | async-start | bytes 1216512 | tf_op jit(solution)/shard_map/all_gather | solution.py:79
  10.4 170.9 %all-gather.10.cloned.1.call-start = ((), (), s32[]{:S(2)}) async-start(), calls=%async_computation.9 | async-start | bytes 1216512 | tf_op jit(solution)/shard_map/all_gather | solution.py:81
  12.0 196.3 %all-gather.16.cloned.1.call-start = ((), (), s32[]{:S(2)}) async-start(), calls=%async_computation.12 | async-start | bytes 1769472 | tf_op jit(solution)/shard_map/all_gather | solution.py:95
  55.8 125.5 %copy-start.29 = (f32[768]{0:T(1024)}, f32[768]{0:T(1024)S(1)}, u32[]{:S(2)}) copy-start(f32[768]{0:T(1024)S(1)} %convert_element_type.141) | copy-start | bytes 9220
  59.7 121.6 %copy-start.44 = (f32[128]{0:T(128)}, f32[128]{0:T(128)S(1)}, u32[]{:S(2)}) copy-start(f32[128]{0:T(128)S(1)} %add_rsqrt_fusion.1) | copy-start | bytes 1540
  127.7 108.5 %all-gather.12.cloned.1.call-start = ((), (), s32[]{:S(2)}) async-start(), calls=%async_computation.10 | async-start | bytes 1769472 | tf_op jit(solution)/shard_map/all_gather | solution.py:96
  183.6 110.1 %all-gather.20.cloned.1.call-start = ((), (), s32[]{:S(2)}) async-start(), calls=%async_computation.14 | async-start | bytes 1216512 | tf_op jit(solution)/shard_map/all_gather | solution.py:137
  184.3 175.4 %all-gather.24.cloned.1.call-start = ((), (), s32[]{:S(2)}) async-start(), calls=%async_computation.16 | async-start | bytes 4866048 | tf_op jit(solution)/shard_map/all_gather | solution.py:145
  185.1 240.6 %all-gather.22.cloned.1.call-start = ((), (), s32[]{:S(2)}) async-start(), calls=%async_computation.15 | async-start | bytes 4866048 | tf_op jit(solution)/shard_map/all_gather | solution.py:144
  185.8 305.9 %all-gather.26.cloned.1.call-start = ((), (), s32[]{:S(2)}) async-start(), calls=%async_computation.17 | async-start | bytes 4866048 | tf_op jit(solution)/shard_map/all_gather | solution.py:155
  186.6 402.1 %reduce-scatter.28.cloned.1.call-start = ((), (), s32[]{:S(2)}) async-start(), calls=%async_computation.25 | async-start | bytes 1769472
  266.0 98.0 %copy-start.47 = (f32[12,1,128]{2,0,1:T(8,128)}, f32[12,1,128]{2,0,1:T(8,128)S(1)}, u32[]{:S(2)}) copy-start(f32[12,1,128]{2,0,1:T(8,128)S(1)} %get-tuple-element.1120) | copy-start | bytes 18436
  295.6 130.2 %copy-start.8 = (bf16[128,768]{1,0:T(8,128)(2,1)}, bf16[128,768]{1,0:T(8,128)(2,1)S(1)}, u32[]{:S(2)}) copy-start(bf16[128,768]{1,0:T(8,128)(2,1)S(1)} %multiply_convert_fusion.4) | copy-start | bytes 589828
  364.0 127.7 %copy-start.24 = (bf16[128,768]{1,0:T(8,128)(2,1)S(1)}, bf16[128,768]{1,0:T(8,128)(2,1)}, u32[]{:S(2)}) copy-start(bf16[128,768]{1,0:T(8,128)(2,1)} %param.33) | copy-start | bytes 589828
  551.3 79.2 %reduce-scatter.30.cloned.1.call-start = ((), (), s32[]{:S(2)}) async-start(), calls=%async_computation.26 | async-start | bytes 1769472
  556.3 178.9 %reduce-scatter.20.cloned.1.call-start = ((), (), s32[]{:S(2)}) async-start(), calls=%async_computation.21 | async-start | bytes 2433024 | tf_op jit(solution)/shard_map/reduce_scatter | solution.py:273
  558.4 281.6 %reduce-scatter.14.cloned.1.call-start = ((), (), s32[]{:S(2)}) async-start(), calls=%async_computation.18 | async-start | bytes 2433024 | tf_op jit(solution)/shard_map/reduce_scatter | solution.py:273
  592.1 351.7 %reduce-scatter.16.cloned.1.call-start = ((), (), s32[]{:S(2)}) async-start(), calls=%async_computation.19 | async-start | bytes 2433024 | tf_op jit(solution)/shard_map/reduce_scatter | solution.py:273
  594.2 454.1 %reduce-scatter.18.cloned.1.call-start = ((), (), s32[]{:S(2)}) async-start(), calls=%async_computation.20 | async-start | bytes 2433024 | tf_op jit(solution)/shard_map/reduce_scatter | solution.py:273
  633.5 555.9 %reduce-scatter.22.cloned.1.call-start = ((), (), s32[]{:S(2)}) async-start(), calls=%async_computation.22 | async-start | bytes 9732096 | tf_op jit(solution)/shard_map/reduce_scatter | solution.py:273
  638.9 692.3 %reduce-scatter.24.cloned.1.call-start = ((), (), s32[]{:S(2)}) async-start(), calls=%async_computation.23 | async-start | bytes 9732096 | tf_op jit(solution)/shard_map/reduce_scatter | solution.py:273
  645.1 827.2 %reduce-scatter.26.cloned.1.call-start = ((), (), s32[]{:S(2)}) async-start(), calls=%async_computation.24 | async-start | bytes 9732096 | tf_op jit(solution)/shard_map/reduce_scatter | solution.py:162
  (59 other events, 777.8 us)
Sparse Core Ops, SparseCore 0:
  11.5 56.7 all-gather.13
  71.8 52.9 all-gather.17
  128.3 52.9 all-gather.9
  183.6 24.6 all-gather.15
  210.5 25.6 all-gather.11
  239.6 54.0 all-gather.19
  297.1 62.5 all-gather.23
  363.2 62.4 all-gather.21
  429.2 62.4 all-gather.25
  551.4 37.2 reduce-scatter.27
  592.0 38.4 reduce-scatter.29
  636.2 98.9 reduce-scatter.19
  741.9 98.0 reduce-scatter.13
  845.7 98.0 reduce-scatter.15
  950.3 97.9 reduce-scatter.17
  1054.6 134.6 reduce-scatter.21
  1196.7 134.4 reduce-scatter.23
  1337.5 134.7 reduce-scatter.25
where the time goes:
time: 1480 us
  waiting for transfers between devices  1210 us (82%)
  matrix products  83.3 us (6%)
  blocking collectives  81.9 us (6%)
  local copies, waits for them, and re-layouts  49.5 us (3%)
  other arithmetic  32.9 us (2%)
  between operations  14.9 us (1%)
    reduce_scatter x6, waiting for transfers between devices, body(): lax.psum_scatter((attn_gain_local, mlp_gain_local, out_term, q_term, k_te...  632 us
    reduce_scatter x1, waiting for transfers between devices, body(): lax.psum_scatter(jnp.einsum('tn,tc->nc', cols, grad_y, preferred_element_...  141 us
    unnamed x2, blocking collectives  81.9 us
    unnamed x20, waiting for transfers between devices  66.9 us
    all_gather x1, waiting for transfers between devices, body(): lax.all_gather(up_weight.astype(jnp.bfloat16), ('dp', 'blk'), axis=0, til...  64.2 us
    all_gather x1, waiting for transfers between devices, body(): lax.all_gather(gate_weight.astype(jnp.bfloat16), ('dp', 'blk'), axis=0, t...  61.7 us
    all_gather x1, waiting for transfers between devices, body(): lax.all_gather(down_weight.astype(jnp.bfloat16), ('dp', 'blk'), axis=0, t...  61.7 us
    all_gather x1, waiting for transfers between devices, body(): lax.all_gather(q_weight.astype(jnp.bfloat16), ('dp', 'blk'), axis=0, tile...  54.5 us
  transfers between devices with their start and end apart: 18, of which 18 were waited for; matrix products, arithmetic and copies ran while one was open for 7% of the time, Pallas kernels for 0%

commit v1 on v0

v1 whole, which is shorter than its diff:
```python
import functools
import math

import jax
import jax.numpy as jnp
import numpy as np
from jax import lax
from jax.experimental import pallas as pl
from jax.experimental.pallas import tpu as pltpu
from jax.sharding import PartitionSpec as P

H = 12
HD = 64
G = 4
HG = H // G
QG = HG * HD
QKV = 3 * QG
QKVP = 640
EPS = 1e-05
THETA = 10000.0
NEG = -1e30
F32 = jnp.float32
BF = jnp.bfloat16
MESH = pl.DeviceIdType.MESH


def dot_nn(a, b):
    return jnp.dot(a, b, preferred_element_type=F32)


def dot_nt(a, b):
    return lax.dot_general(a, b, (((1,), (1,)), ((), ())), preferred_element_type=F32)


class Place:
    def __init__(self, cf):
        self.cf = cf
        self.d = lax.axis_index("dp")
        self.b = lax.axis_index("blk")
        self.g = self.b // cf.S
        self.s = lax.rem(self.b, cf.S)

    def in_plane(self, k):
        return (self.d, jnp.bitwise_xor(self.g, k) * self.cf.S + self.s)

    def along_z(self, k):
        return (jnp.bitwise_xor(self.d, k), self.b)

    def in_group(self, k):
        return (self.d, self.g * self.cf.S + jnp.bitwise_xor(self.s, k))


class Net:
    def __init__(self, send_sem, recv_sem):
        self.send_sem, self.recv_sem, self.copies = send_sem, recv_sem, []

    def send(self, src, dst, device):
        at = len(self.copies)
        copy = pltpu.make_async_remote_copy(
            src_ref=src,
            dst_ref=dst,
            send_sem=self.send_sem.at[at],
            recv_sem=self.recv_sem.at[at],
            device_id=device,
            device_id_type=MESH,
        )
        copy.start()
        self.copies.append(copy)
        return copy

    def finish(self):
        for copy in self.copies:
            copy.wait_send()


def arrive(copies):
    for copy in copies:
        copy.wait_recv()


def greet(cf, me):
    barrier = pltpu.get_barrier_semaphore()
    peers = [me.in_plane(k) for k in range(1, G)]
    peers += [me.along_z(k) for k in range(1, cf.nd)]
    peers += [me.in_group(k) for k in range(1, cf.S)]
    for peer in peers:
        pl.semaphore_signal(barrier, inc=1, device_id=peer, device_id_type=MESH)
    pl.semaphore_wait(barrier, len(peers))


def keep_column(keep_ref):
    n = keep_ref.shape[1]
    rows = lax.broadcasted_iota(jnp.int32, (n, n), 0)
    lanes = lax.broadcasted_iota(jnp.int32, (n, n), 1)
    keep = keep_ref[...].astype(F32)
    return jnp.sum(jnp.where(rows == lanes, keep, 0.0), axis=1, keepdims=True)


def row_to_column(row):
    n = row.shape[1]
    rows = lax.broadcasted_iota(jnp.int32, (n, n), 0)
    lanes = lax.broadcasted_iota(jnp.int32, (n, n), 1)
    return jnp.sum(jnp.where(rows == lanes, row, 0.0), axis=1, keepdims=True)


def column_to_row(column):
    n = column.shape[0]
    rows = lax.broadcasted_iota(jnp.int32, (n, n), 0)
    lanes = lax.broadcasted_iota(jnp.int32, (n, n), 1)
    return jnp.sum(jnp.where(rows == lanes, column, 0.0), axis=0, keepdims=True)


def doc_begin(len_ref, pos):
    begin = jnp.int32(0)
    start = jnp.int32(0)
    for e in range(len_ref.shape[1]):
        begin = jnp.where(start <= pos, start, begin)
        start = start + len_ref[0, e]
    return begin


def rotary(cf, len_ref, tab_m, tab_r, c):
    pos = c * cf.T
    m = (pos - doc_begin(len_ref, pos)) // cf.T
    cm, sm = tab_m[0, pl.ds(m, 1), :], tab_m[1, pl.ds(m, 1), :]
    cr, sr = tab_r[0], tab_r[1]
    cosine = cm * cr - sm * sr
    sine = sm * cr + cm * sr
    lane = lax.broadcasted_iota(jnp.int32, sine.shape, 1)
    return cosine, jnp.where(lane % HD < HD // 2, -sine, sine)


def swap_halves(slab):
    lane = lax.broadcasted_iota(jnp.int32, slab.shape, 1)
    half = HD // 2
    return jnp.where(lane % HD < half, pltpu.roll(slab, 128 - half, 1), pltpu.roll(slab, half, 1))


def turn(heads, cosine, sine):
    padded = jnp.concatenate([heads, jnp.zeros((heads.shape[0], 256 - QG), F32)], axis=1)
    slabs = [padded[:, at : at + 128] for at in (0, 128)]
    return jnp.concatenate([slab * cosine + swap_halves(slab) * sine for slab in slabs], axis=1)


def kernel_a(
    cf, x_ref, cot_ref, keep_ref, len_ref, g1_ref, g2_ref, wq, wk, wv, wo, wg, wu, tab_m, tab_r,
    WQ, W2, WOF, DYG, XG, XN1, QH, KV, LSE, MIX, HS, XN2, G12,
    W1, WO, PK1, PK2, VT, OH, OS, OX, ssem, rsem,
):
    me = Place(cf)
    d, g, s = me.d, me.g, me.s
    T, S, nd, D = cf.T, cf.S, cf.nd, cf.D
    net = Net(ssem, rsem)
    greet(cf, me)

    gains = jnp.concatenate(
        [row_to_column(g1_ref[...]), row_to_column(g2_ref[...]), jnp.zeros((cf.R, QKVP - QKV - 2), F32)],
        axis=1,
    )
    for t in range(G):
        at = t * QG
        PK1[t] = jnp.concatenate(
            [w[:, at : at + QG] for w in (wq, wk, wv)] + [gains], axis=1
        ).astype(BF)
    W1[d, g, s] = PK1[g]
    first = [net.send(PK1.at[jnp.bitwise_xor(g, k)], W1.at[d, g, s], me.in_plane(k)) for k in (1, 2, 3)]
    XG[g] = x_ref[...]
    tokens = [net.send(x_ref, XG.at[g], me.in_plane(k)) for k in (1, 2, 3)]
    for t in range(G):
        PK2[t] = jnp.concatenate(
            [
                w[:, (G * p + t) * cf.FB : (G * p + t + 1) * cf.FB]
                for w in (wg, wu)
                for p in range(nd)
            ],
            axis=1,
        ).astype(BF)
    W2[d, g, s] = PK2[g]
    second = [net.send(PK2.at[jnp.bitwise_xor(g, k)], W2.at[d, g, s], me.in_plane(k)) for k in (1, 2, 3)]

    arrive(first)
    first_z = [net.send(W1.at[d, :, s], W1.at[d, :, s], me.along_z(k)) for k in range(1, nd)]
    WO[d, g, s] = wo[...].astype(BF)
    out_z = [net.send(WO.at[d, g, s], WO.at[d, g, s], me.along_z(k)) for k in range(1, nd)]
    keep = keep_column(keep_ref)
    DYG[g] = (keep * cot_ref[...].astype(F32)).astype(BF)
    grads = [net.send(DYG.at[g], DYG.at[g], me.in_plane(k)) for k in (1, 2, 3)]
    arrive(second)
    second_z = [net.send(W2.at[d, :, s], W2.at[d, :, s], me.along_z(k)) for k in range(1, nd)]
    arrive(first_z)
    first_s = [net.send(W1.at[:, :, s], W1.at[:, :, s], me.in_group(k)) for k in range(1, S)]
    arrive(out_z)
    out_p = [net.send(WO.at[:, g, s], WO.at[:, g, s], me.in_plane(k)) for k in (1, 2, 3)]
    arrive(first_s)
    WQ[...] = W1[...].reshape(D, QKVP)
    arrive(tokens)
    turned = jnp.transpose(WQ[:, QKVP - 128 : QKVP].astype(F32))
    row = QKV - (QKVP - 128)
    G12[...] = turned[row : row + 8, :]
    gain1 = G12[0:1, :]

    def project(j, unused):
        c = j * S + s
        inputs = XG[j].astype(F32)
        scale1 = lax.rsqrt(jnp.mean(inputs * inputs, axis=-1, keepdims=True) + EPS)
        normed = (inputs * scale1 * gain1).astype(BF)
        XN1[j] = normed
        acc = dot_nn(normed, WQ[...])
        cosine, sine = rotary(cf, len_ref, tab_m, tab_r, c)
        q = turn(acc[:, :QG], cosine, sine).astype(BF)
        k = turn(acc[:, QG : 2 * QG], cosine, sine).astype(BF)
        v = acc[:, 2 * QG : QKV].astype(BF)
        here = pl.ds(pl.multiple_of(c * T, T), T)
        mine = pl.ds(pl.multiple_of(j * T, T), T)
        for h in range(HG):
            QH[h, mine, :] = q[:, h * HD : (h + 1) * HD]
            KV[h, here, :] = k[:, h * HD : (h + 1) * HD]
            KV[HG + h, here, :] = v[:, h * HD : (h + 1) * HD]
        return unused

    lax.fori_loop(0, G, project, 0)
    rows = [
        (c, net.send(KV.at[:, pl.ds(pl.multiple_of((j * S + s) * T, T), T), :],
                     KV.at[:, pl.ds(pl.multiple_of((j * S + s) * T, T), T), :], me.in_group(k)))
        for k in range(1, S) for j in range(G) for c in (0,)
    ]
    arrive(out_p)
    out_s = [net.send(WO.at[:, :, s], WO.at[:, :, s], me.in_group(k)) for k in range(1, S)]
    arrive([copy for unused, copy in rows])

    def attend(h, unused):
        VT[...] = jnp.transpose(KV[HG + h])
        for j in range(G):
            c = j * S + s
            length = (j + 1) * S * T
            begin = doc_begin(len_ref, c * T)
            raw = dot_nt(KV[h, :length, :], QH[h, j * T : (j + 1) * T, :]) * cf.scale
            kpos = lax.broadcasted_iota(jnp.int32, raw.shape, 0)
            qpos = lax.broadcasted_iota(jnp.int32, raw.shape, 1) + c * T
            raw = jnp.where((kpos <= qpos) & (kpos >= begin), raw, NEG)
            top = jnp.max(raw, axis=0, keepdims=True)
            expo = jnp.exp(raw - top)
            total = jnp.sum(expo, axis=0, keepdims=True)
            probs = (expo * (1.0 / total)).astype(BF)
            LSE[h, 0:1, j * T : (j + 1) * T] = top + jnp.log(total)
            mixed = dot_nn(VT[:, :length], probs)
            OH[h, j * T : (j + 1) * T, :] = jnp.transpose(mixed).astype(BF)
        return unused

    lax.fori_loop(0, HG, attend, 0)
    for j in range(G):
        OS[j] = jnp.concatenate([OH[h, j * T : (j + 1) * T, :] for h in range(HG)], axis=1)
    OX[g] = OS[g]
    heads = [net.send(OS.at[jnp.bitwise_xor(g, k)], OX.at[g], me.in_plane(k)) for k in (1, 2, 3)]
    arrive(out_s)
    WOF[...] = WO[...].reshape(D, D)
    arrive(heads)
    MIX[...] = jnp.concatenate([OX[t] for t in range(G)], axis=1)
    state = x_ref[...].astype(F32) + keep * dot_nn(MIX[...], WOF[...])
    HS[...] = state
    scale2 = lax.rsqrt(jnp.mean(state * state, axis=-1, keepdims=True) + EPS)
    XN2[...] = (state * scale2 * G12[1:2, :]).astype(BF)
    arrive(second_z)
    second_s = [net.send(W2.at[:, :, s], W2.at[:, :, s], me.in_group(k)) for k in range(1, S)]
    arrive(grads)
    arrive(second_s)
    net.finish()


def kernel_b(
    cf, XN2, DYG, W2, wd, HS, cot_ref, keep_ref, G12, WOF, MIX,
    YS, YO, DH, DO, GU, GD, GO, MG,
    X2G, WD, WDF, HID, DGU, XT, HT, MT, DXF, DXS, RDX, ssem, rsem,
):
    me = Place(cf)
    d, g, s = me.d, me.g, me.s
    T, S, nd, D, FG = cf.T, cf.S, cf.nd, cf.D, cf.FG
    TT = G * T
    net = Net(ssem, rsem)
    greet(cf, me)
    X2G[g] = XN2[...]
    acts = [net.send(XN2, X2G.at[g], me.in_plane(k)) for k in (1, 2, 3)]
    WD[d, s] = wd[...].astype(BF)
    down_z = [net.send(WD.at[d, s], WD.at[d, s], me.along_z(k)) for k in range(1, nd)]
    keep = keep_column(keep_ref)
    arrive(down_z)
    down_s = [net.send(WD.at[:, s], WD.at[:, s], me.in_group(k)) for k in range(1, S)]
    arrive(acts)
    arrive(down_s)
    WDF[...] = WD[...].reshape(FG, D)

    def tile(n):
        return pl.ds(pl.multiple_of(n * 256, 256), 256)

    def middle(n, unused):
        x = X2G[...].reshape(TT, D)
        gate = dot_nn(x, W2[:, tile(n)])
        up = dot_nn(x, W2[:, tile(n + FG // 256)])
        dhid = dot_nt(DYG[...].reshape(TT, D), WDF[tile(n), :])
        sig = jax.nn.sigmoid(gate)
        HID[:, tile(n)] = (gate * sig * up).astype(BF)
        DGU[:, tile(n)] = (dhid * up * sig * (1.0 + gate * (1.0 - sig))).astype(BF)
        DGU[:, tile(n + FG // 256)] = (dhid * gate * sig).astype(BF)
        return unused

    lax.fori_loop(0, FG // 256, middle, 0)

    def back(n, unused):
        part = dot_nt(DGU[...], W2[tile(n), :])
        DXF[:, tile(n)] = part
        DXS[:, :, tile(n)] = part.astype(BF).reshape(G, T, 256)
        return unused

    lax.fori_loop(0, D // 256, back, 0)
    sums = [net.send(DXS.at[jnp.bitwise_xor(g, k)], RDX.at[k - 1], me.in_plane(k)) for k in (1, 2, 3)]

    XT[...] = jnp.transpose(X2G[...].reshape(TT, D))
    HT[...] = jnp.transpose(HID[...])
    MT[...] = jnp.transpose(MIX[...])

    def weight_grads(n, unused):
        GU[:, tile(n)] = dot_nn(XT[...], DGU[:, tile(n)]).astype(BF)
        return unused

    lax.fori_loop(0, 2 * FG // 256, weight_grads, 0)

    def down_grads(n, unused):
        GD[:, tile(n)] = dot_nn(HT[...], DYG[:, :, tile(n)].reshape(TT, 256)).astype(BF)
        y = dot_nn(HID[...], WDF[:, tile(n)])
        YS[:, :, tile(n)] = y.astype(BF).reshape(G, T, 256)
        return unused

    lax.fori_loop(0, D // 256, down_grads, 0)
    mine = pl.ds(pl.multiple_of(g * T, T), T)
    YO[...] = dot_nn(HID[mine, :], WDF[...])

    arrive(sums)
    dxn2 = DXF[mine, :]
    for k in (1, 2, 3):
        dxn2 = dxn2 + RDX[k - 1].astype(F32)
    state = HS[...]
    scale2 = lax.rsqrt(jnp.mean(state * state, axis=-1, keepdims=True) + EPS)
    hhat = state * scale2
    MG[...] = jnp.broadcast_to(jnp.sum(dxn2 * hhat, axis=0, keepdims=True), MG.shape)
    dhh = dxn2 * G12[1:2, :]
    dh = cot_ref[...].astype(F32) + scale2 * (dhh - hhat * jnp.mean(dhh * hhat, axis=-1, keepdims=True))
    DH[...] = dh
    da = (keep * dh).astype(BF)
    DO[...] = dot_nt(da, WOF[...]).astype(BF)
    GO[...] = dot_nn(MT[...], da).astype(BF)
    net.finish()


def kernel_c(
    cf, x_ref, keep_ref, len_ref, tab_m, tab_r, WQ, XG, XN1, QH, KV, LSE, HS, G12, YS, YO, DH, DO, GU, GD, GO, MG,
    layer_out, tokens_grad, ga, gq, gk, gv, go, gm, gg, gu, gd,
    DOS, DOG, DOH, RY, RGU, RGD, RGO, ZGU, ZGD, NGO, ZGO, OGU, OGO, KT, DKV, DQ, DKS, RDK, DQKV, DXF, DXS, RDX,
    XT, GQ, RGQ, ZGQ, OGQ, ssem, rsem,
):
    me = Place(cf)
    d, g, s = me.d, me.g, me.s
    T, S, nd, D, R, FG, FB = cf.T, cf.S, cf.nd, cf.D, cf.R, cf.FG, cf.FB
    TT = G * T
    net = Net(ssem, rsem)
    other = lambda k: jnp.bitwise_xor(g, k)
    plane = lambda k: jnp.bitwise_xor(d, k)
    sub = lambda k: jnp.bitwise_xor(s, k)
    greet(cf, me)
    do = DO[...]
    for t in range(G):
        DOS[t] = do[:, t * QG : (t + 1) * QG]
    DOG[g] = DOS[g]
    heads = [net.send(DOS.at[other(k)], DOG.at[g], me.in_plane(k)) for k in (1, 2, 3)]
    subs = range(1, S)
    pair_u = [net.send(GU.at[:, :, sub(k)], RGU.at[k - 1], me.in_group(k)) for k in subs]
    pair_d = [net.send(GD.at[:, sub(k)], RGD.at[k - 1], me.in_group(k)) for k in subs]
    pair_o = [net.send(GO.at[:, :, sub(k)], RGO.at[k - 1], me.in_group(k)) for k in subs]
    outs = [net.send(YS.at[other(k)], RY.at[k - 1], me.in_plane(k)) for k in (1, 2, 3)]

    arrive(pair_u)

    def add_u(i, unused):
        p, t = i // G, lax.rem(i, G)
        total = GU[p, t, s].astype(F32)
        for k in subs:
            total = total + RGU[k - 1, p, t].astype(F32)
        RGU[0, p, t] = total.astype(BF)
        return unused

    lax.fori_loop(0, nd * G, add_u, 0)
    z_u = [net.send(RGU.at[0, plane(k)], ZGU.at[k - 1], me.along_z(k)) for k in range(1, nd)]
    arrive(pair_d)

    def add_d(p, unused):
        total = GD[p, s].astype(F32)
        for k in subs:
            total = total + RGD[k - 1, p].astype(F32)
        RGD[0, p] = total.astype(BF)
        return unused

    lax.fori_loop(0, nd, add_d, 0)
    z_d = [net.send(RGD.at[0, plane(k)], ZGD.at[k - 1], me.along_z(k)) for k in range(1, nd)]
    arrive(pair_o)

    def add_o(i, unused):
        p, t = i // G, lax.rem(i, G)
        total = GO[p, t, s].astype(F32)
        for k in subs:
            total = total + RGO[k - 1, p, t].astype(F32)
        RGO[0, p, t] = total.astype(BF)
        return unused

    lax.fori_loop(0, nd * G, add_o, 0)
    plane_o = [net.send(RGO.at[0, :, other(k)], NGO.at[k - 1], me.in_plane(k)) for k in (1, 2, 3)]

    arrive(heads)
    for j in range(G):
        for h in range(HG):
            DOH[h, j * T : (j + 1) * T, :] = DOG[j, :, h * HD : (h + 1) * HD]

    def attend(h, unused):
        KT[...] = jnp.transpose(KV[h])
        for j in range(G - 1, -1, -1):
            c = j * S + s
            length = (j + 1) * S * T
            mine = slice(j * T, (j + 1) * T)
            begin = doc_begin(len_ref, c * T)
            q, dout = QH[h, mine, :], DOH[h, mine, :]
            raw = dot_nt(KV[h, :length, :], q) * cf.scale
            kpos = lax.broadcasted_iota(jnp.int32, raw.shape, 0)
            qpos = lax.broadcasted_iota(jnp.int32, raw.shape, 1) + c * T
            allow = (kpos <= qpos) & (kpos >= begin)
            probs = jnp.where(allow, jnp.exp(raw - LSE[h, 0:1, mine]), 0.0)
            dprobs = dot_nt(KV[HG + h, :length, :], dout)
            delta = jnp.sum(probs * dprobs, axis=0, keepdims=True)
            dscores = (probs * (dprobs - delta) * cf.scale).astype(BF)
            dk = dot_nn(dscores, q)
            dv = dot_nn(probs.astype(BF), dout)
            if j < G - 1:
                dk = dk + DKV[h, :length, :]
                dv = dv + DKV[HG + h, :length, :]
            DKV[h, :length, :] = dk
            DKV[HG + h, :length, :] = dv
            DQ[h, mine, :] = jnp.transpose(dot_nn(KT[:, :length], dscores))
        return unused

    lax.fori_loop(0, HG, attend, 0)
    for k in subs:
        for j in range(G):
            rows = pl.ds(pl.multiple_of((j * S + sub(k)) * T, T), T)
            DKS[k - 1, :, j * T : (j + 1) * T, :] = DKV[:, rows, :].astype(BF)
    pair_k = [net.send(DKS.at[k - 1], RDK.at[k - 1], me.in_group(k)) for k in subs]
    XT[...] = jnp.transpose(XN1[...].reshape(TT, D))

    arrive(plane_o)

    def sum_o(p, unused):
        total = RGO[0, p, g].astype(F32)
        for k in (1, 2, 3):
            total = total + NGO[k - 1, p].astype(F32)
        OGO[p] = total.astype(BF)
        return unused

    lax.fori_loop(0, nd, sum_o, 0)
    z_o = [net.send(OGO.at[plane(k)], ZGO.at[k - 1], me.along_z(k)) for k in range(1, nd)]

    arrive(pair_k)
    for j in range(G):
        c = j * S + s
        rows = pl.ds(pl.multiple_of(c * T, T), T)
        mine = slice(j * T, (j + 1) * T)
        cosine, sine = rotary(cf, len_ref, tab_m, tab_r, c)
        whole = []
        for h in range(2 * HG):
            total = DKV[h, rows, :]
            for k in subs:
                total = total + RDK[k - 1, h, mine, :].astype(F32)
            whole.append(total)
        dq = jnp.concatenate([DQ[h, mine, :] for h in range(HG)], axis=1)
        dq = turn(dq, cosine, -sine)[:, :QG]
        dk = turn(jnp.concatenate(whole[:HG], axis=1), cosine, -sine)[:, :QG]
        DQKV[mine, :] = jnp.concatenate(
            [dq, dk] + whole[HG:] + [jnp.zeros((T, QKVP - QKV), F32)], axis=1
        ).astype(BF)

    def tile(n):
        return pl.ds(pl.multiple_of(n * 256, 256), 256)

    def back(n, unused):
        part = dot_nt(DQKV[...], WQ[tile(n), :])
        DXF[:, tile(n)] = part
        DXS[:, :, tile(n)] = part.astype(BF).reshape(G, T, 256)
        return unused

    lax.fori_loop(0, D // 256, back, 0)
    sums = [net.send(DXS.at[other(k)], RDX.at[k - 1], me.in_plane(k)) for k in (1, 2, 3)]

    def gain(j, total):
        inputs = XG[j].astype(F32)
        scale1 = lax.rsqrt(jnp.mean(inputs * inputs, axis=-1, keepdims=True) + EPS)
        part = DXF[pl.ds(pl.multiple_of(j * T, T), T), :]
        return total + jnp.sum(part * (inputs * scale1), axis=0, keepdims=True)

    gain_row = lax.fori_loop(0, G, gain, jnp.zeros((1, D), F32))
    spare = QKV - (QKVP - 128)
    rows = lax.broadcasted_iota(jnp.int32, (128, D), 0)
    gain_rows = jnp.where(rows == spare, gain_row, jnp.where(rows == spare + 1, MG[0:1, :], 0.0))
    products = [dot_nn(XT[...], DQKV[:, at : at + 128]) for at in range(0, QKVP, 128)]
    products[-1] = products[-1] + jnp.transpose(gain_rows)
    GQ[...] = jnp.concatenate([p.astype(BF) for p in products], axis=1).reshape(nd, G, S, R, QKVP)
    pair_q = [net.send(GQ.at[:, :, sub(k)], RGQ.at[k - 1], me.in_group(k)) for k in subs]
    arrive(pair_q)

    def add_q(i, unused):
        p, t = i // G, lax.rem(i, G)
        total = GQ[p, t, s].astype(F32)
        for k in subs:
            total = total + RGQ[k - 1, p, t].astype(F32)
        RGQ[0, p, t] = total.astype(BF)
        return unused

    lax.fori_loop(0, nd * G, add_q, 0)
    z_q = [net.send(RGQ.at[0, plane(k)], ZGQ.at[k - 1], me.along_z(k)) for k in range(1, nd)]

    arrive(z_u)

    def total_u(t, unused):
        total = RGU[0, d, t].astype(F32)
        for k in range(1, nd):
            total = total + ZGU[k - 1, t].astype(F32)
        OGU[t] = total.astype(BF)
        return unused

    def stage_u(t, unused):
        total = RGU[0, d, t].astype(F32)
        for k in range(1, nd):
            total = total + ZGU[k - 1, t].astype(F32)
        ZGU[0, t] = total.astype(BF)
        return unused

    del total_u
    lax.fori_loop(0, G, stage_u, 0)
    OGU[g] = ZGU[0, g]
    plane_u = [net.send(ZGU.at[0, other(k)], OGU.at[g], me.in_plane(k)) for k in (1, 2, 3)]
    arrive(z_d)
    total = RGD[0, d].astype(F32)
    for k in range(1, nd):
        total = total + ZGD[k - 1].astype(F32)
    gd[...] = total
    arrive(z_o)
    total = OGO[d].astype(F32)
    for k in range(1, nd):
        total = total + ZGO[k - 1].astype(F32)
    go[...] = total

    keep = keep_column(keep_ref)
    arrive(outs)
    y = YO[...]
    for k in (1, 2, 3):
        y = y + RY[k - 1].astype(F32)
    layer_out[...] = (HS[...] + keep * y).astype(BF)
    arrive(sums)
    mine = pl.ds(pl.multiple_of(g * T, T), T)
    dxn1 = DXF[mine, :]
    for k in (1, 2, 3):
        dxn1 = dxn1 + RDX[k - 1].astype(F32)
    inputs = x_ref[...].astype(F32)
    scale1 = lax.rsqrt(jnp.mean(inputs * inputs, axis=-1, keepdims=True) + EPS)
    unit = inputs * scale1
    dxx = dxn1 * G12[0:1, :]
    tokens_grad[...] = (
        DH[...] + scale1 * (dxx - unit * jnp.mean(dxx * unit, axis=-1, keepdims=True))
    ).astype(BF)

    arrive(plane_u)
    for at, out in ((0, gg), (FG, gu)):
        out[...] = jnp.concatenate(
            [OGU[t, :, at + p * FB : at + (p + 1) * FB].astype(F32) for p in range(nd) for t in range(G)],
            axis=1,
        )
    arrive(z_q)

    def stage_q(t, unused):
        total = RGQ[0, d, t].astype(F32)
        for k in range(1, nd):
            total = total + ZGQ[k - 1, t].astype(F32)
        ZGQ[0, t] = total.astype(BF)
        return unused

    lax.fori_loop(0, G, stage_q, 0)
    OGQ[g] = ZGQ[0, g]
    plane_q = [net.send(ZGQ.at[0, other(k)], OGQ.at[g], me.in_plane(k)) for k in (1, 2, 3)]
    arrive(plane_q)
    parts = [OGQ[t].astype(F32) for t in range(G)]
    for at, out in ((0, gq), (QG, gk), (2 * QG, gv)):
        out[...] = jnp.concatenate([part[:, at : at + QG] for part in parts], axis=1)
    both = parts[0] + parts[1] + parts[2] + parts[3]
    ga[...] = column_to_row(both[:, QKV : QKV + 1])
    gm[...] = column_to_row(both[:, QKV + 1 : QKV + 2])
    net.finish()


class Sizes:
    pass


def tables(cf):
    lanes = np.arange(128) % (HD // 2)
    freq = THETA ** (-2.0 * lanes / HD)
    coarse = np.arange(cf.row_len // cf.T)[:, None] * cf.T * freq[None, :]
    fine = np.arange(cf.T)[:, None] * freq[None, :]
    stack = lambda a: np.stack([np.cos(a), np.sin(a)]).astype(np.float32)
    return stack(coarse), stack(fine)


def vmem(shape, dtype=BF):
    return jax.ShapeDtypeStruct(shape, dtype)


def call(kernel, cf, name, collective, outs, scratch, n_sems, args, smem=()):
    in_specs = [
        pl.BlockSpec(memory_space=pltpu.SMEM if i in smem else pltpu.VMEM) for i in range(len(args))
    ]
    return pl.pallas_call(
        functools.partial(kernel, cf),
        out_shape=[jax.ShapeDtypeStruct(shape, dtype) for shape, dtype in outs],
        in_specs=in_specs,
        out_specs=[pl.BlockSpec(memory_space=pltpu.VMEM) for unused in outs],
        scratch_shapes=[pltpu.VMEM(shape, dtype) for shape, dtype in scratch]
        + [pltpu.SemaphoreType.DMA((n_sems,)), pltpu.SemaphoreType.DMA((n_sems,))],
        compiler_params=pltpu.CompilerParams(collective_id=collective, has_side_effects=True),
        name=name,
    )(*args)


def body(
    nd, nb, tokens, attn_gain, q_weight, k_weight, v_weight, o_weight, mlp_gain, gate_weight, up_weight,
    down_weight, doc_lengths, keep, cotangent,
):
    cf = Sizes()
    cf.nd, cf.S = nd, nb // G
    cf.T, cf.D = tokens.shape
    cf.R, cf.RF = q_weight.shape[0], down_weight.shape[0]
    cf.FF = gate_weight.shape[1]
    cf.FG, cf.FB = cf.FF // G, cf.FF // (G * nd)
    cf.row_len = cf.T * nb
    cf.scale = 1.0 / math.sqrt(HD)
    T, D, S, R, RF, FG = cf.T, cf.D, cf.S, cf.R, cf.RF, cf.FG
    TT = G * T
    tab_m, tab_r = tables(cf)
    keep_row = keep.reshape(1, T)
    rows = (nd, G, S, R)
    many = 16 + 9 * nd + 12 * S

    WQ, W2, WOF, DYG, XG, XN1, QH, KV, LSE, MIX, HS, XN2, G12 = call(
        kernel_a, cf, "forward_attention", 0,
        [((D, QKVP), BF), (rows + (2 * FG,), BF), ((D, D), BF), ((G, T, D), BF), ((G, T, D), BF), ((G, T, D), BF),
         ((HG, TT, HD), BF), ((2 * HG, cf.row_len, HD), BF), ((HG, 8, TT), F32), ((T, D), BF), ((T, D), F32),
         ((T, D), BF), ((8, D), F32)],
        [(rows + (QKVP,), BF), (rows + (D,), BF), ((G, R, QKVP), BF), ((G, R, 2 * FG), BF), ((HD, cf.row_len), BF),
         ((HG, TT, HD), BF), ((G, T, QG), BF), ((G, T, QG), BF)],
        many,
        [tokens, cotangent, keep_row, doc_lengths, attn_gain.reshape(1, R), mlp_gain.reshape(1, R), q_weight,
         k_weight, v_weight, o_weight, gate_weight, up_weight, tab_m, tab_r],
        smem=(3,),
    )
    YS, YO, DH, DO, GU, GD, GO, MG = call(
        kernel_b, cf, "feed_forward", 1,
        [((G, T, D), BF), ((T, D), F32), ((T, D), F32), ((T, D), BF), ((D, 2 * FG), BF), ((FG, D), BF), ((D, D), BF),
         ((8, D), F32)],
        [((G, T, D), BF), ((nd, S, RF, D), BF), ((FG, D), BF), ((TT, FG), BF), ((TT, 2 * FG), BF), ((D, TT), BF),
         ((FG, TT), BF), ((D, T), BF), ((TT, D), F32), ((G, T, D), BF), ((3, T, D), BF)],
        many,
        [XN2, DYG, W2.reshape(D, 2 * FG), down_weight, HS, cotangent, keep_row, G12, WOF, MIX],
    )
    layer_out, tokens_grad, ga, gq, gk, gv, go, gm, gg, gu, gd = call(
        kernel_c, cf, "backward_attention", 2,
        [((T, D), BF), ((T, D), BF), ((1, R), F32), ((R, D), F32), ((R, D), F32), ((R, D), F32), ((R, D), F32),
         ((1, R), F32), ((R, cf.FF), F32), ((R, cf.FF), F32), ((RF, D), F32)],
        [((G, T, QG), BF), ((G, T, QG), BF), ((HG, TT, HD), BF), ((3, T, D), BF),
         ((S - 1, nd, G, R, 2 * FG), BF), ((S - 1, nd, RF, D), BF), ((S - 1, nd, G, R, D), BF),
         ((nd - 1, G, R, 2 * FG), BF), ((nd - 1, RF, D), BF), ((3, nd, R, D), BF), ((nd - 1, R, D), BF),
         ((G, R, 2 * FG), BF), ((nd, R, D), BF), ((HD, cf.row_len), BF), ((2 * HG, cf.row_len, HD), F32),
         ((HG, TT, HD), F32), ((S - 1, 2 * HG, TT, HD), BF), ((S - 1, 2 * HG, TT, HD), BF), ((TT, QKVP), BF),
         ((TT, D), F32), ((G, T, D), BF), ((3, T, D), BF), ((D, TT), BF), (rows + (QKVP,), BF),
         ((S - 1, nd, G, R, QKVP), BF), ((nd - 1, G, R, QKVP), BF), ((G, R, QKVP), BF)],
        many,
        [tokens, keep_row, doc_lengths, tab_m, tab_r, WQ, XG, XN1, QH, KV, LSE, HS, G12, YS, YO, DH, DO,
         GU.reshape(rows + (2 * FG,)), GD.reshape(nd, S, RF, D), GO.reshape(rows + (D,)), MG],
        smem=(2,),
    )
    return (
        layer_out, tokens_grad, ga.reshape(R), gq, gk, gv, go, gm.reshape(R), gg, gu, gd,
    )


def solution(mesh):
    both = ("dp", "blk")
    rows, flat = P(both, None), P(both)
    in_specs = (
        rows, flat, rows, rows, rows, rows, flat, rows, rows, rows, P("dp", None), flat, rows,
    )
    out_specs = (rows, rows, flat, rows, rows, rows, rows, flat, rows, rows, rows)
    step = functools.partial(body, mesh.shape["dp"], mesh.shape["blk"])
    return jax.shard_map(step, mesh=mesh, in_specs=in_specs, out_specs=out_specs, check_vma=False)
```

time: 1480 us -> 181 us (0.12)
  waiting for transfers between devices: 1210 us -> 0 us
  Pallas kernels: 0 us -> 166 us
  matrix products: 83.3 us -> 0 us
  blocking collectives: 81.9 us -> 0 us
  local copies, waits for them, and re-layouts: 49.5 us -> 13.9 us
  other arithmetic: 32.9 us -> 0 us
    reduce_scatter x7 -> x0, waiting for transfers between devices: 773 us -> none  [the longest x6 632 us: body(): lax.psum_scatter((attn_gain_local, mlp_gain_local, out_term, q_term, k_te...]
    all_gather x9 -> x0, waiting for transfers between devices: 375 us -> none  [the longest x1 64.2 us: body(): lax.all_gather(up_weight.astype(jnp.bfloat16), ('dp', 'blk'), axis=0, til...]
    pallas_call x0 -> x3, Pallas kernels: none -> 166 us  [call(): pl.pallas_call(functools.partial(kernel, cf), out_shape=[jax.ShapeDtypeSt...]
    dot_general x39 -> x0, matrix products: 83.3 us -> none  [the longest x1 6.06 us: body(): jnp.einsum('tc,nc->tn', grad_y, down_whole, preferred_element_type=jnp.fl...]
    unnamed x2 -> x0, blocking collectives: 81.9 us -> none
    unnamed x20 -> x0, waiting for transfers between devices: 66.9 us -> none
    dynamic_slice x16 -> x0, local copies, waits for them, and re-layouts: 22.1 us -> none  [body(): lax.scan(stats_step, start_stats, (key_blocks, block_starts))]
  transfers between devices with their start and end apart: 18 -> 0, of which waited for: 18 -> 0; matrix products, arithmetic and copies ran while one was open for 7% -> 0% of each run, Pallas kernels for 0% -> 0%
where the time goes in v1:
time: 181 us; the launch traced here: 180 us
  Pallas kernels  166 us (92%)
  local copies, waits for them, and re-layouts  13.9 us (8%)
    pallas_call x3, Pallas kernels, call(): pl.pallas_call(functools.partial(kernel, cf), out_shape=[jax.ShapeDtypeSt...  166 us
    unnamed x17, local copies, waits for them, and re-layouts  13.9 us

profile of v1, /device:TPU:0, one launch (start us, length us, event | category | flops | bytes accessed | tf_op | source)
XLA Modules:
  0.0 180.5 jit_solution(8912075545082228983)
XLA Ops:
  0.6 54.1 %forward_attention.1 = (bf16[768,640]{1,0:T(8,128)(2,1)}, bf16[4,4,2,24,1536]{4,3,2,1,0:T(8,128)(2,1)}, bf16[768,768]{1,0:T(8,128)(2,1)}, bf16[4,128,768]{2,1,0:...) custom-call(bf16[128,768]{1,0:T(8,128)(2,1)} %x_ref.3, ...), custom_call_target="tpu_custom_call" | custom-call | tf_op jit(solution)/shard_map/forward_attention/pallas_call | solution.py:624
  54.8 41.6 %feed_forward.1 = (bf16[4,128,768]{2,1,0:T(8,128)(2,1)}, f32[128,768]{1,0:T(8,128)}, f32[128,768]{1,0:T(8,128)}, bf16[128,768]{1,0:T(8,128)(2,1)}, bf16[768,1536...) custom-call(bf16[128,768]{1,0:T(8,128)(2,1)} %get-tuple-element.51.XN2, ...), custom_call_target="tpu_custom_call" | custom-call | tf_op jit(solution)/shard_map/feed_forward/pallas_call | solution.py:624
  96.4 70.1 %backward_attention.1 = (bf16[128,768]{1,0:T(8,128)(2,1)}, bf16[128,768]{1,0:T(8,128)(2,1)}, f32[1,24]{1,0:T(1,128)}, f32[24,768]{1,0:T(8,128)}, f32[24,768]{1,0...) custom-call(bf16[128,768]{1,0:T(8,128)(2,1)} %x_ref.3, ...), custom_call_target="tpu_custom_call" | custom-call | tf_op jit(solution)/shard_map/backward_attention/pallas_call | solution.py:624
  166.6 0.0 copy-start.2
  166.6 0.0 copy-start.1
  166.6 0.0 copy-start
  166.6 1.7 copy.37
  168.3 1.6 copy.38
  169.9 1.2 copy.39
  171.1 1.5 copy.40
  172.6 1.5 copy.41
  174.1 1.5 copy.42
  175.7 1.5 copy.43
  177.2 1.2 copy.44
  178.3 0.0 copy-done.2
  178.3 0.7 copy.45
  179.1 0.0 copy-done.1
  179.1 0.7 copy.46
  179.8 0.0 copy-done
  179.8 0.7 copy.47
Async XLA Ops:
  166.6 11.8 %copy-start.2 = (f32[24,3072]{1,0:T(8,128)S(1)}, f32[24,3072]{1,0:T(8,128)}, u32[]{:S(2)}) copy-start(f32[24,3072]{1,0:T(8,128)} %get-tuple-element.94) | copy-start | bytes 884740
  166.6 12.5 %copy-start.1 = (f32[24,3072]{1,0:T(8,128)S(1)}, f32[24,3072]{1,0:T(8,128)}, u32[]{:S(2)}) copy-start(f32[24,3072]{1,0:T(8,128)} %get-tuple-element.95) | copy-start | bytes 884740
  166.6 13.2 %copy-start = (f32[96,768]{1,0:T(8,128)S(1)}, f32[96,768]{1,0:T(8,128)}, u32[]{:S(2)}) copy-start(f32[96,768]{1,0:T(8,128)} %get-tuple-element.96) | copy-start | bytes 884740
